TPU v7x, 512 devices: a whole 4x8x8 slice. The times are simulated.
512 devices in a mesh: gx: 32 (over y, x), gy: 16 (over z, core).
Axes of the slice: x: 4, y: 8, z: 8, core: 2. Of those that a mesh axis runs over, the one named last changes fastest.
Arguments:
- diag_blocks: float32 [9, 2048, 2048], P(None, 'gx', 'gy'), may hold values from 0 to 36, as said below
- edge_blocks: float32 [4, 9, 2048, 2048], P(None, None, 'gx', 'gy'), may hold values from -0.3 to 0.3
- edge_mask: int32 [4, 2048, 2048], P(None, 'gx', 'gy'), may hold values 0 or 1
- src_values: float32 [3, 524288], P(None, ('gx', 'gy')), may hold values from -48 to 48
- src_owner: int32 [524288, 1], P(('gx', 'gy')), may hold values from 0 to 31; in each aligned block of 1024 rows (0 to 1023, 1024 to 2047, ...) at most 64 rows name the same one
- src_node: int32 [524288], P(('gx', 'gy')), may hold values from 0 to 8191
- src_count: int32 [512], P(('gx', 'gy')), may hold values from 256 to 1024, as said below
- surf_node: int32 [1048576], P(('gx', 'gy')), may hold values from 0 to 8191
- surf_param: float32 [3, 1048576], P(None, ('gx', 'gy')), may hold values from 0 to 1
- tile_box: int32 [8192], P(('gx', 'gy')), may hold values from 0 to 511
Outputs:
- adjoint_field: float32 [3, 2048, 2048], P(None, 'gx', 'gy')
- box_gradient: float32 [512, 192], P(('gx', 'gy'))
Inputs may be any that keep to these rules, and one draw needn't show every extreme that they name: `src_owner`: each device's rows name every gx index at most 64 times. `src_count`: some device has all 1024 rows live. `diag_blocks`: entries 0, 4 and 8 lie between 6 and 36; the other entries between 0 and 1.
All inputs are finite; a program needn't handle non-finite values. No bound on the sum of `edge_mask` on one device may be relied on, other than what follows from the above.
Results may differ from a plain program's by a relative error of at most 0.0015.
Values sent between devices are 32-bit elements; how exact they have to be, the bound alone decides.
A program may use at most 64 MiB of HBM per device.

v0:
```python
import jax
import jax.numpy as jnp
from jax import lax
from jax.sharding import PartitionSpec as P

ITERS = 2


def passed_along(block, axis, distance):
    devices = range(lax.axis_size(axis))
    route = [(i - distance, i) for i in devices if i - distance in devices]
    return lax.ppermute(block, axis, route)


def block_product(blocks, field):
    return jnp.stack(
        [
            blocks[row] * field[0] + blocks[3 + row] * field[1] + blocks[6 + row] * field[2]
            for row in range(3)
        ]
    )


def apply_transposed_operator(field, diag_blocks, masked):
    result = block_product(diag_blocks, field)
    toward_upx = block_product(masked[0], field)
    toward_lowx = block_product(masked[1], field)
    toward_upy = block_product(masked[2], field)
    toward_lowy = block_product(masked[3], field)
    from_below_x = passed_along(toward_upx[:, -1:, :], "gx", 1)
    upper_x = jnp.concatenate([from_below_x, toward_upx[:, :-1, :]], axis=1)
    from_above_x = passed_along(toward_lowx[:, :1, :], "gx", -1)
    lower_x = jnp.concatenate([toward_lowx[:, 1:, :], from_above_x], axis=1)
    from_below_y = passed_along(toward_upy[:, :, -1:], "gy", 1)
    upper_y = jnp.concatenate([from_below_y, toward_upy[:, :, :-1]], axis=2)
    from_above_y = passed_along(toward_lowy[:, :, :1], "gy", -1)
    lower_y = jnp.concatenate([toward_lowy[:, :, 1:], from_above_y], axis=2)
    return result + upper_x + lower_x + upper_y + lower_y


def bernstein(coord):
    other = 1.0 - coord
    return jnp.stack(
        [
            other * other * other,
            3.0 * coord * other * other,
            3.0 * coord * coord * other,
            coord * coord * coord,
        ]
    )


def tile_weights(params):
    first = bernstein(params[0])
    second = bernstein(params[1])
    third = bernstein(params[2])
    table = first[:, None, None, :] * second[None, :, None, :] * third[None, None, :, :]
    return table.reshape(64, -1)


def residual_sum(residual, precond):
    return lax.psum(jnp.sum(residual * precond), ("gx", "gy"))


def per_device(
    diag_blocks,
    edge_blocks,
    edge_mask,
    src_values,
    src_owner,
    src_node,
    src_count,
    surf_node,
    surf_param,
    tile_box,
):
    masked = edge_blocks * edge_mask.astype(jnp.float32)[:, None]
    cells_x = diag_blocks.shape[1]
    cells_y = diag_blocks.shape[2]
    rows = src_node.shape[0]
    flat_load = jnp.zeros((3, cells_x * cells_y), jnp.float32)
    all_values, every_owner_index, all_node, all_count = (
        lax.all_gather(src_values, "gx", axis=1, tiled=True),
        lax.all_gather(src_owner, "gx", axis=0, tiled=True),
        lax.all_gather(src_node, "gx", axis=0, tiled=True),
        lax.all_gather(src_count, "gx", axis=0, tiled=True),
    )
    position = jnp.arange(all_node.shape[0], dtype=jnp.int32)
    live = position % rows < jnp.repeat(all_count, rows)
    keeper = live & (every_owner_index[:, 0] == lax.axis_index("gx"))
    flat_load = flat_load.at[:, all_node].add(all_values * keeper.astype(jnp.float32))
    load = flat_load.reshape(3, cells_x, cells_y)
    scale = jnp.stack([diag_blocks[0], diag_blocks[4], diag_blocks[8]])
    solution = jnp.zeros_like(load)
    residual = load
    precond = residual / scale
    search = precond
    norm_now = residual_sum(residual, precond)
    for sweep in range(ITERS):
        image = apply_transposed_operator(search, diag_blocks, masked)
        step_size = norm_now / lax.psum(jnp.sum(search * image), ("gx", "gy"))
        solution = solution + step_size * search
        residual = residual - step_size * image
        if sweep + 1 < ITERS:
            precond = residual / scale
            norm_next = residual_sum(residual, precond)
            search = precond + norm_next / norm_now * search
            norm_now = norm_next
    design_sensitivity = solution.reshape(3, -1)[:, surf_node]
    tile_weight_values = tile_weights(surf_param)
    surface_tiles = tile_box.shape[0]
    series_terms = jnp.einsum(
        "bqe,iqe->qib",
        tile_weight_values.reshape(64, surface_tiles, -1),
        design_sensitivity.reshape(3, surface_tiles, -1),
        precision=lax.Precision.HIGHEST,
    ).reshape(surface_tiles, 192)
    box_count = lax.axis_size("gx") * lax.axis_size("gy")
    onehot = (jnp.arange(box_count, dtype=jnp.int32)[:, None] == tile_box[None, :]).astype(
        jnp.float32
    )
    partial_boxes = jnp.dot(onehot, series_terms, precision=lax.Precision.HIGHEST)
    totals = lax.psum(partial_boxes, ("gx", "gy"))
    gradient = lax.dynamic_slice_in_dim(totals, lax.axis_index(("gx", "gy")), 1, 0)
    return (solution, gradient)


def solution(mesh):
    return jax.shard_map(
        per_device,
        mesh=mesh,
        in_specs=(
            P(None, "gx", "gy"),
            P(None, None, "gx", "gy"),
            P(None, "gx", "gy"),
            P(None, ("gx", "gy")),
            P(("gx", "gy"), None),
            P(("gx", "gy")),
            P(("gx", "gy")),
            P(("gx", "gy")),
            P(None, ("gx", "gy")),
            P(("gx", "gy")),
        ),
        out_specs=(P(None, "gx", "gy"), P(("gx", "gy"), None)),
        check_vma=False,
    )
```

profile of v0, /device:TPU:24, one launch (start us, length us, event | category | flops | bytes accessed | tf_op | source)
XLA Modules:
  0.0 972.0 jit_solution(12247643676694862051)
XLA Ops:
  7.2 39.1 %all_gather.15 = s32[32768,1]{0,1:T(1,128)S(1)} all-gather(s32[1024,1]{0,1:T(1,128)} %param.14), channel_id=1, replica_groups=mesh['gx'=32,'gy'=16] {'gx'}, dimensions={0}, use_global_device_ids=true | all-gather | bytes 135168 | tf_op jit(solution)/shard_map/all_gather | solution.py:84
  46.9 1.3 dynamic-slice
  48.2 0.8 dynamic-update-slice
  49.0 17.6 %all-reduce = s32[32]{0:T(128)S(1)} all-reduce(s32[32]{0:T(128)S(1)} %dynamic-update-slice), channel_id=1, replica_groups=mesh['gx'=32,'gy'=16] {'gx'}, use_global_device_ids=true, to_apply=%add | all-reduce | flops 32 | bytes 256
  66.7 48.2 %all_gather.13 = f32[3,32768]{1,0:T(4,128)S(1)} all-gather(f32[3,1024]{1,0:T(4,128)} %param.13), channel_id=1, replica_groups=mesh['gx'=32,'gy'=16] {'gx'}, dimensions={1}, use_global_device_ids=true | all-gather | bytes 405504 | tf_op jit(solution)/shard_map/all_gather | solution.py:83
  114.9 0.4 compare_reduce_fusion
  115.3 0.1 multiply_bitcast_fusion
  115.5 8.6 copy.63
  124.1 36.8 %all_gather.12 = s32[32768]{0:T(1024)S(1)} all-gather(s32[1024]{0:T(1024)S(1)} %copy-done.6), channel_id=1, replica_groups=mesh['gx'=32,'gy'=16] {'gx'}, dimensions={0}, use_global_device_ids=true | all-gather | bytes 135168 | tf_op jit(solution)/shard_map/all_gather | solution.py:85
  160.9 176.4 %scatter_custom_fusion = f32[3,8192]{0,1:T(8,128)} fusion(s32[32768]{0:T(1024)S(1)} %compare_select_fusion, f32[32768,3]{1,0:T(8,128)} %copy.63, f32[]{:T(128)} %constant.12.clone.1), kind=kCustom, calls=%fused_computation.2 | custom fusion | flops 98304 | bytes 98816 | tf_op jit(solution)/shard_map/scatter-add | solution.py:91
  337.3 3.0 copy.66
  340.3 0.1 broadcast_multiply_fusion
  340.5 0.6 pad_maximum_fusion.21
  341.1 2.5 collective-permute-start
  343.6 0.6 pad_maximum_fusion.20
  344.2 5.5 collective-permute-start.1
  349.7 0.7 slice.525
  350.5 1.3 collective-permute-start.2
  351.8 1.3 collective-permute-start.3
  353.1 0.7 multiply_add_fusion.32
  354.0 0.1 broadcast_multiply_fusion.1
  354.1 0.1 slice.536
  354.2 2.8 copy.65
  357.1 0.3 mul.732
  357.4 0.1 fusion.28
  357.6 0.1 fusion.27
  357.7 1.8 multiply_reduce_fusion.1
  359.6 105.4 %all-reduce.1 = (f32[]{:T(128)}, f32[]{:T(128)}) all-reduce(f32[]{:T(128)} %get-tuple-element.3, f32[]{:T(128)} %get-tuple-element.2), channel_id=1, replica_groups=mesh['gx'=32,'gy'=16] {'gx','gy'}, use_global_device_ids=true, to_apply=%region_2.3 | all-reduce | flops 2 | bytes 16 | tf_op jit(solution)/shard_map/psum | solution.py:62
  466.3 0.7 multiply_reduce_fusion
  467.0 96.2 %psum.37 = f32[]{:T(128)} all-reduce(f32[]{:T(128)} %get-tuple-element.6), channel_id=1, replica_groups=mesh['gx'=32,'gy'=16] {'gx','gy'}, use_global_device_ids=true, to_apply=%region_6.7 | all-reduce | flops 1 | bytes 8 | tf_op jit(solution)/shard_map/psum | solution.py:62
  564.5 0.9 fusion.21
  565.6 3.1 collective-permute-start.4
  568.8 4.9 collective-permute-start.5
  573.7 1.6 collective-permute-start.6
  575.5 1.3 collective-permute-start.7
  576.8 0.1 maximum_bitcast_fusion.1
  576.9 1.8 collective-permute-done.7
  578.7 0.1 maximum_bitcast_fusion.2
  578.8 0.9 fusion.7
  579.7 100.5 %psum.38 = f32[]{:T(128)} all-reduce(f32[]{:T(128)} %fusion.7), channel_id=1, replica_groups=mesh['gx'=32,'gy'=16] {'gx','gy'}, use_global_device_ids=true, to_apply=%region_8.9 | all-reduce | flops 1 | bytes 8 | tf_op jit(solution)/shard_map/psum | solution.py:101
  681.6 2.6 copy.69
  684.2 7.7 gather_fusion
  691.9 1.8 fusion.2
  693.7 0.1 reshape.251
  693.8 1.2 fusion.4
  695.0 0.7 multiply_add_fusion.2
  695.7 268.2 %all-reduce.4.cloned.1.call-done = f32[512,192]{1,0:T(8,128)} async-done(((f32[512,192]{1,0:T(8,128)}), f32[512,192]{1,0:T(8,128)}) %all-reduce.4.cloned.1.call-update) | async-done | bytes 393232 | tf_op jit(solution)/shard_map/psum | solution.py:123
  963.9 1.3 constant_dynamic-slice_fusion
  (64 shorter events, 1.2 us)
Async XLA Ops:
  7.2 956.7 %all-reduce.4.cloned.1.call-start = ((), (), s32[]{:S(2)}) async-start(), calls=%async_computation | async-start | bytes 1048576 | tf_op jit(solution)/shard_map/psum | solution.py:123
  115.5 8.6 copy-start.6
  337.3 3.0 copy-start
  337.3 3.0 copy-start.3
  337.3 3.0 copy-start.1
  341.1 16.6 %collective-permute-start = (f32[3,1,128]{2,1,0:T(1,128)}, f32[3,1,128]{2,1,0:T(1,128)S(1)}, u32[]{:S(2)}, u32[]{:S(2)}) collective-permute-start(f32[3,1,128]{2,1,0:T(1,128)} %pad_maximum_fusion.21), channel_id=1, source_target_pairs={{0,16},{16,32},{32,48},{48,64},{64,80},{80,96},{96,112},{112,128},... | collective-permute-start | bytes 4616 | tf_op jit(solution)/shard_map/ppermute | solution.py:12
  343.6 10.2 %copy-start.5 = (s32[2048]{0:T(1024)S(1)}, s32[2048]{0:T(1024)}, u32[]{:S(2)}) copy-start(s32[2048]{0:T(1024)} %param.17) | copy-start | bytes 24580
  343.6 10.1 %copy-start.4 = (f32[3,2048]{1,0:T(4,128)S(1)}, f32[3,2048]{1,0:T(4,128)}, u32[]{:S(2)}) copy-start(f32[3,2048]{1,0:T(4,128)} %param.18) | copy-start | bytes 73732
  344.2 13.5 %collective-permute-start.1 = (f32[3,1,128]{2,1,0:T(1,128)}, f32[3,1,128]{2,1,0:T(1,128)S(1)}, u32[]{:S(2)}, u32[]{:S(2)}) collective-permute-start(f32[3,1,128]{2,1,0:T(1,128)} %pad_maximum_fusion.20), channel_id=1, source_target_pairs={{16,0},{32,16},{48,32},{64,48},{80,64},{96,80},{112,96},{128,112},... | collective-permute-start | bytes 4616 | tf_op jit(solution)/shard_map/ppermute | solution.py:12
  350.5 6.9 collective-permute-start.2
  351.8 5.8 collective-permute-start.3
  357.4 207.1 %copy-start.2 = (f32[1,64,128]{2,1,0:T(8,128)S(1)}, f32[1,64,128]{2,1,0:T(8,128)}, u32[]{:S(2)}) copy-start(f32[1,64,128]{2,1,0:T(8,128)} %get-tuple-element.37) | copy-start | bytes 98308
  565.6 13.1 %collective-permute-start.4 = (f32[3,1,128]{2,1,0:T(1,128)S(1)}, f32[3,1,128]{2,1,0:T(1,128)S(1)}, u32[]{:S(2)}, u32[]{:S(2)}) collective-permute-start(f32[3,1,128]{2,1,0:T(1,128)S(1)} %pad_maximum_fusion.19), channel_id=1, source_target_pairs={{0,16},{16,32},{32,48},{48,64},{64,80},{80,96},{96,112},{112,128},... | collective-permute-start | bytes 4616 | tf_op jit(solution)/shard_map/ppermute | solution.py:12
  568.8 10.0 %collective-permute-start.5 = (f32[3,1,128]{2,1,0:T(1,128)S(1)}, f32[3,1,128]{2,1,0:T(1,128)S(1)}, u32[]{:S(2)}, u32[]{:S(2)}) collective-permute-start(f32[3,1,128]{2,1,0:T(1,128)S(1)} %pad_maximum_fusion.18), channel_id=1, source_target_pairs={{16,0},{32,16},{48,32},{64,48},{80,64},{96,80},{112,96},{128,112},... | collective-permute-start | bytes 4616 | tf_op jit(solution)/shard_map/ppermute | solution.py:12
  573.7 3.0 collective-permute-start.6
  575.5 3.2 collective-permute-start.7
  684.2 9.6 copy-start.7
Sparse Core Ops, SparseCore 0:
  695.1 268.6 all-reduce.3
where the time goes:
time: 973 us; the launch traced here: 972 us
  blocking collectives  444 us (46%)
  waiting for transfers between devices  270 us (28%)
  other arithmetic  185 us (19%)
  local copies, waits for them, and re-layouts  29.5 us (3%)
  starting transfers between devices  21.4 us (2%)
  between operations  19.3 us (2%)
    psum x1, waiting for transfers between devices, per_device(): totals = lax.psum(partial_boxes, ('gx', 'gy'))  268 us
    psum x2, blocking collectives, residual_sum(): return lax.psum(jnp.sum(residual * precond), ('gx', 'gy'))  202 us
    scatter-add x1, other arithmetic, per_device(): flat_load.at[:, all_node].add(all_values * keeper.astype(jnp.float32))  176 us
    psum x1, blocking collectives, per_device(): step_size = norm_now / lax.psum(jnp.sum(search * image), ('gx', 'gy'))  100 us
    all_gather x1, blocking collectives, per_device(): lax.all_gather(src_values, 'gx', axis=1, tiled=True)  48.2 us
    all_gather x1, blocking collectives, per_device(): lax.all_gather(src_owner, 'gx', axis=0, tiled=True)  39.1 us
    all_gather x1, blocking collectives, per_device(): lax.all_gather(src_node, 'gx', axis=0, tiled=True)  36.8 us
    ppermute x8, starting transfers between devices, passed_along(): return lax.ppermute(block, axis, route)  21.4 us
  transfers between devices with their start and end apart: 9, of which 3 were waited for; matrix products, arithmetic and copies ran while one was open for 1% of the time, Pallas kernels for 0%

commit v1 on v0

--- a/solution.py
+++ b/solution.py
@@ -120,7 +120,8 @@
         jnp.float32
     )
     partial_boxes = jnp.dot(onehot, series_terms, precision=lax.Precision.HIGHEST)
-    totals = lax.psum(partial_boxes, ("gx", "gy"))
+    z = lax.psum(partial_boxes, axis_name="gx")
+    totals = lax.psum(z, "gy")
     gradient = lax.dynamic_slice_in_dim(totals, lax.axis_index(("gx", "gy")), 1, 0)
     return (solution, gradient)
 

time: 973 us -> 974 us (level)
  the two profiles are of different devices: /device:TPU:24 before, /device:TPU:1 now
where the time goes in v1:
time: 974 us; the launch traced here: 973 us
  blocking collectives  411 us (42%)
  waiting for transfers between devices  276 us (28%)
  other arithmetic  182 us (19%)
  starting transfers between devices  52.3 us (5%)
  local copies, waits for them, and re-layouts  28.9 us (3%)
  between operations  19.3 us (2%)
    psum x2, blocking collectives, residual_sum(): return lax.psum(jnp.sum(residual * precond), ('gx', 'gy'))  201 us
    scatter-add x1, other arithmetic, per_device(): flat_load.at[:, all_node].add(all_values * keeper.astype(jnp.float32))  176 us
    psum x1, waiting for transfers between devices, per_device(): z = lax.psum(partial_boxes, axis_name='gx')  153 us
    psum x1, waiting for transfers between devices, per_device(): totals = lax.psum(z, 'gy')  119 us
    psum x1, blocking collectives, per_device(): step_size = norm_now / lax.psum(jnp.sum(search * image), ('gx', 'gy'))  99.6 us
    ppermute x8, starting transfers between devices, passed_along(): return lax.ppermute(block, axis, route)  52.2 us
    all_gather x1, blocking collectives, per_device(): lax.all_gather(src_values, 'gx', axis=1, tiled=True)  36 us
    all_gather x1, blocking collectives, per_device(): lax.all_gather(src_owner, 'gx', axis=0, tiled=True)  32.4 us
  transfers between devices with their start and end apart: 10, of which 4 were waited for; matrix products, arithmetic and copies ran while one was open for 0% of the time, Pallas kernels for 0%

profile of v1, /device:TPU:1, one launch (start us, length us, event | category | flops | bytes accessed | tf_op | source)
XLA Modules:
  0.0 973.2 jit_solution(2934652766072731491)
XLA Ops:
  7.2 32.4 %all_gather.15 = s32[32768,1]{0,1:T(1,128)S(1)} all-gather(s32[1024,1]{0,1:T(1,128)} %param.14), channel_id=1, replica_groups=mesh['gx'=32,'gy'=16] {'gx'}, dimensions={0}, use_global_device_ids=true | all-gather | bytes 135168 | tf_op jit(solution)/shard_map/all_gather | solution.py:84
  40.3 1.3 dynamic-slice
  41.5 0.8 dynamic-update-slice
  42.3 13.0 %all-reduce = s32[32]{0:T(128)S(1)} all-reduce(s32[32]{0:T(128)S(1)} %dynamic-update-slice), channel_id=1, replica_groups=mesh['gx'=32,'gy'=16] {'gx'}, use_global_device_ids=true, to_apply=%add | all-reduce | flops 32 | bytes 256
  55.4 36.0 %all_gather.13 = f32[3,32768]{1,0:T(4,128)S(1)} all-gather(f32[3,1024]{1,0:T(4,128)} %param.13), channel_id=1, replica_groups=mesh['gx'=32,'gy'=16] {'gx'}, dimensions={1}, use_global_device_ids=true | all-gather | bytes 405504 | tf_op jit(solution)/shard_map/all_gather | solution.py:83
  91.4 0.4 compare_reduce_fusion
  91.8 0.1 multiply_bitcast_fusion
  92.0 8.6 copy.63
  100.6 29.8 %all_gather.12 = s32[32768]{0:T(1024)S(1)} all-gather(s32[1024]{0:T(1024)S(1)} %copy-done.5), channel_id=1, replica_groups=mesh['gx'=32,'gy'=16] {'gx'}, dimensions={0}, use_global_device_ids=true | all-gather | bytes 135168 | tf_op jit(solution)/shard_map/all_gather | solution.py:85
  130.4 176.4 %scatter_custom_fusion = f32[3,8192]{0,1:T(8,128)} fusion(s32[32768]{0:T(1024)S(1)} %compare_select_fusion, f32[32768,3]{1,0:T(8,128)} %copy.63, f32[]{:T(128)} %constant.12.clone.1), kind=kCustom, calls=%fused_computation.2 | custom fusion | flops 98304 | bytes 98816 | tf_op jit(solution)/shard_map/scatter-add | solution.py:91
  306.8 3.0 copy.66
  309.8 0.1 broadcast_multiply_fusion
  310.1 1.9 collective-permute-start
  312.1 1.3 collective-permute-start.1
  313.5 0.1 slice.525
  313.6 37.0 %collective-permute-start.2 = (f32[3,64,1]{2,1,0:T(8,128)S(1)}, f32[3,64,1]{2,1,0:T(8,128)S(1)}, u32[]{:S(2)}, u32[]{:S(2)}) collective-permute-start(f32[3,64,1]{2,1,0:T(8,128)S(1)} %slice.525), channel_id=1, source_target_pairs={{0,1},{1,2},{2,3},{3,4},{4,5},{5,6},{6,7},{7,8},{8,9},{9,10},{10,1... | collective-permute-start | bytes 2312 | tf_op jit(solution)/shard_map/ppermute | solution.py:12
  350.6 1.9 collective-permute-start.3
  352.8 0.1 broadcast_multiply_fusion.1
  353.0 0.1 slice.536
  353.1 2.8 copy.65
  356.0 0.1 fusion.28
  356.1 0.5 collective-permute-done.3
  356.5 0.1 fusion.27
  356.7 1.1 multiply_reduce_fusion.1
  357.8 104.9 %all-reduce.1 = (f32[]{:T(128)}, f32[]{:T(128)}) all-reduce(f32[]{:T(128)} %get-tuple-element.3, f32[]{:T(128)} %get-tuple-element.2), channel_id=1, replica_groups=mesh['gx'=32,'gy'=16] {'gx','gy'}, use_global_device_ids=true, to_apply=%region_2.3 | all-reduce | flops 2 | bytes 16 | tf_op jit(solution)/shard_map/psum | solution.py:62
  464.1 0.7 multiply_reduce_fusion
  464.8 95.7 %psum.44 = f32[]{:T(128)} all-reduce(f32[]{:T(128)} %get-tuple-element.6), channel_id=1, replica_groups=mesh['gx'=32,'gy'=16] {'gx','gy'}, use_global_device_ids=true, to_apply=%region_6.7 | all-reduce | flops 1 | bytes 8 | tf_op jit(solution)/shard_map/psum | solution.py:62
  561.9 0.1 fusion.21
  562.3 2.7 collective-permute-start.4
  565.0 1.3 collective-permute-start.5
  566.3 0.1 slice.542
  566.4 4.1 collective-permute-start.6
  570.6 1.9 collective-permute-start.7
  572.5 0.1 maximum_bitcast_fusion.1
  572.6 3.9 collective-permute-done.7
  576.5 0.1 maximum_bitcast_fusion.2
  576.7 0.9 fusion.7
  577.6 0.3 mul.732
  577.9 99.6 %psum.45 = f32[]{:T(128)} all-reduce(f32[]{:T(128)} %fusion.7), channel_id=1, replica_groups=mesh['gx'=32,'gy'=16] {'gx','gy'}, use_global_device_ids=true, to_apply=%region_8.9 | all-reduce | flops 1 | bytes 8 | tf_op jit(solution)/shard_map/psum | solution.py:101
  678.9 2.6 copy.69
  681.5 7.7 gather_fusion
  689.2 1.8 fusion.2
  691.0 0.1 reshape.251
  691.1 1.1 fusion.4
  692.3 152.7 %all-reduce.5.cloned.1.call-done = f32[512,192]{1,0:T(8,128)} async-done(((f32[512,192]{1,0:T(8,128)}), f32[512,192]{1,0:T(8,128)}) %all-reduce.5.cloned.1.call-update) | async-done | bytes 393232 | tf_op jit(solution)/shard_map/psum | solution.py:123
  845.0 0.7 multiply_add_fusion.2
  845.7 119.4 %all-reduce.7.cloned.1.call-done = f32[512,192]{1,0:T(8,128)} async-done(((f32[512,192]{1,0:T(8,128)}), f32[512,192]{1,0:T(8,128)}) %all-reduce.7.cloned.1.call-update) | async-done | bytes 393232 | tf_op jit(solution)/shard_map/psum | solution.py:124
  965.1 1.3 constant_dynamic-slice_fusion
  (65 shorter events, 1.1 us)
Async XLA Ops:
  7.2 837.9 %all-reduce.5.cloned.1.call-start = ((), (), s32[]{:S(2)}) async-start(), calls=%async_computation | async-start | bytes 1048576 | tf_op jit(solution)/shard_map/psum | solution.py:123
  92.0 8.6 copy-start.5
  306.8 3.0 copy-start
  306.8 3.0 copy-start.2
  306.8 3.0 copy-start.1
  310.1 46.6 %collective-permute-start = (f32[3,1,128]{2,1,0:T(1,128)S(1)}, f32[3,1,128]{2,1,0:T(1,128)S(1)}, u32[]{:S(2)}, u32[]{:S(2)}) collective-permute-start(f32[3,1,128]{2,1,0:T(1,128)S(1)} %pad_maximum_fusion.21), channel_id=1, source_target_pairs={{0,16},{16,32},{32,48},{48,64},{64,80},{80,96},{96,112},{112,128},... | collective-permute-start | bytes 4616 | tf_op jit(solution)/shard_map/ppermute | solution.py:12
  312.1 40.5 %copy-start.4 = (s32[2048]{0:T(1024)S(1)}, s32[2048]{0:T(1024)}, u32[]{:S(2)}) copy-start(s32[2048]{0:T(1024)} %param.17) | copy-start | bytes 24580
  312.1 40.5 %copy-start.3 = (f32[3,2048]{1,0:T(4,128)S(1)}, f32[3,2048]{1,0:T(4,128)}, u32[]{:S(2)}) copy-start(f32[3,2048]{1,0:T(4,128)} %param.18) | copy-start | bytes 73732
  312.1 44.6 %collective-permute-start.1 = (f32[3,1,128]{2,1,0:T(1,128)S(1)}, f32[3,1,128]{2,1,0:T(1,128)S(1)}, u32[]{:S(2)}, u32[]{:S(2)}) collective-permute-start(f32[3,1,128]{2,1,0:T(1,128)S(1)} %pad_maximum_fusion.20), channel_id=1, source_target_pairs={{16,0},{32,16},{48,32},{64,48},{80,64},{96,80},{112,96},{128,112},... | collective-permute-start | bytes 4616 | tf_op jit(solution)/shard_map/ppermute | solution.py:12
  313.6 42.4 %collective-permute-start.2 = (f32[3,64,1]{2,1,0:T(8,128)S(1)}, f32[3,64,1]{2,1,0:T(8,128)S(1)}, u32[]{:S(2)}, u32[]{:S(2)}) collective-permute-start(f32[3,64,1]{2,1,0:T(8,128)S(1)} %slice.525), channel_id=1, source_target_pairs={{0,1},{1,2},{2,3},{3,4},{4,5},{5,6},{6,7},{7,8},{8,9},{9,10},{10,1... | collective-permute-start | bytes 2312 | tf_op jit(solution)/shard_map/ppermute | solution.py:12
  350.6 5.9 collective-permute-start.3
  562.3 14.4 %collective-permute-start.4 = (f32[3,1,128]{2,1,0:T(1,128)S(1)}, f32[3,1,128]{2,1,0:T(1,128)S(1)}, u32[]{:S(2)}, u32[]{:S(2)}) collective-permute-start(f32[3,1,128]{2,1,0:T(1,128)S(1)} %pad_maximum_fusion.19), channel_id=1, source_target_pairs={{0,16},{16,32},{32,48},{48,64},{64,80},{80,96},{96,112},{112,128},... | collective-permute-start | bytes 4616 | tf_op jit(solution)/shard_map/ppermute | solution.py:12
  565.0 11.7 %collective-permute-start.5 = (f32[3,1,128]{2,1,0:T(1,128)S(1)}, f32[3,1,128]{2,1,0:T(1,128)S(1)}, u32[]{:S(2)}, u32[]{:S(2)}) collective-permute-start(f32[3,1,128]{2,1,0:T(1,128)S(1)} %pad_maximum_fusion.18), channel_id=1, source_target_pairs={{16,0},{32,16},{48,32},{64,48},{80,64},{96,80},{112,96},{128,112},... | collective-permute-start | bytes 4616 | tf_op jit(solution)/shard_map/ppermute | solution.py:12
  566.4 6.1 collective-permute-start.6
  570.6 5.9 collective-permute-start.7
  681.5 9.6 copy-start.6
  692.3 272.8 %all-reduce.7.cloned.1.call-start = ((), (), s32[]{:S(2)}) async-start(), calls=%async_computation.1 | async-start | bytes 1048576 | tf_op jit(solution)/shard_map/psum | solution.py:124
Sparse Core Ops, SparseCore 0:
  692.4 152.5 all-reduce.4
  847.4 117.5 all-reduce.6
